TPU v7x, 128 devices: a whole 4x4x4 slice. The times are simulated.
128 devices in a mesh: fsdp: 16 (over x_lo, y, core), tp: 8 (over x_hi, z).
Axes of the slice: x: 4 (x_hi: 2, x_lo: 2; x = x_hi * 2 + x_lo), y: 4, z: 4, core: 2. Of those that a mesh axis runs over, the one named last changes fastest.
Arguments:
- tokens: bfloat16 [16384, 2048], P(('fsdp', 'tp')), may hold values from -6 to 6
- grad_out: bfloat16 [16384, 2048], P(('fsdp', 'tp')), may hold values from -6 to 6
- adapter_ids: int32 [16], P('fsdp'), may hold values from 0 to 7
- first_gain: float32 [2048], replicated, may hold values from 0.1 to 1.9
- first_shift: float32 [2048], replicated, may hold values from -4 to 4
- joined_weight: bfloat16 [2048, 6144], P('fsdp', 'tp'), may hold values from -0.125 to 0.125
- joined_bias: float32 [6144], P('tp'), may hold values from -4 to 4
- dense_weight: bfloat16 [2048, 2048], P('tp', 'fsdp'), may hold values from -0.5 to 0.5
- dense_bias: float32 [2048], replicated, may hold values from -4 to 4
- second_gain: float32 [2048], replicated, may hold values from 0.1 to 1.9
- second_shift: float32 [2048], replicated, may hold values from -4 to 4
- up_weight: bfloat16 [2048, 8192], P('fsdp', 'tp'), may hold values from -0.125 to 0.125
- up_bias: float32 [8192], P('tp'), may hold values from -6 to 6
- down_weight: bfloat16 [8192, 2048], P('tp', 'fsdp'), may hold values from -0.125 to 0.125
- down_bias: float32 [2048], replicated, may hold values from -4 to 4
- joined_adapt_in: bfloat16 [8, 2048, 16], replicated, may hold values from -0.125 to 0.125
- joined_adapt_out: bfloat16 [8, 16, 6144], P(None, None, 'tp'), may hold values from -2 to 2
- dense_adapt_in: bfloat16 [8, 2048, 16], P(None, 'tp'), may hold values from -0.5 to 0.5
- dense_adapt_out: bfloat16 [8, 16, 2048], replicated, may hold values from -2 to 2
- up_adapt_in: bfloat16 [8, 2048, 16], replicated, may hold values from -0.125 to 0.125
- up_adapt_out: bfloat16 [8, 16, 8192], P(None, None, 'tp'), may hold values from -2 to 2
- down_adapt_in: bfloat16 [8, 8192, 16], P(None, 'tp'), may hold values from -0.125 to 0.125
- down_adapt_out: bfloat16 [8, 16, 2048], replicated, may hold values from -2 to 2
Outputs:
- layer_out: bfloat16 [16384, 2048], P(('fsdp', 'tp'))
- grad_tokens: float32 [16384, 2048], P(('fsdp', 'tp'))
- grad_joined_in: float32 [8, 2048, 16], replicated
- grad_joined_out: float32 [8, 16, 6144], P(None, None, 'tp')
- grad_dense_in: float32 [8, 2048, 16], P(None, 'tp')
- grad_dense_out: float32 [8, 16, 2048], replicated
- grad_up_in: float32 [8, 2048, 16], replicated
- grad_up_out: float32 [8, 16, 8192], P(None, None, 'tp')
- grad_down_in: float32 [8, 8192, 16], P(None, 'tp')
- grad_down_out: float32 [8, 16, 2048], replicated
All inputs are finite; a program needn't handle non-finite values.
Results may differ from a plain program's by a relative error of at most 0.02.
Values may be sent and summed in bfloat16 or wider, within the bound.
A program may use at most 128 MiB of HBM per device.

v0:
```python
import jax
import jax.numpy as jnp
from jax import lax
from jax.sharding import PartitionSpec as P

HEADS = 32
HEAD_DIM = 64
EPSILON = 1e-05
MASKED = -1e30
HIGHEST = lax.Precision.HIGHEST


def split_up(value, dim, size):
    before, after = (value.shape[:dim], value.shape[dim + 1 :])
    return jnp.moveaxis(value.reshape(*before, size, -1, *after), dim, 0)


def sum_at_owner(value, axis, dim):
    blocks = split_up(value, dim, lax.axis_size(axis))
    arrived = lax.all_to_all(blocks, axis, split_axis=0, concat_axis=0, tiled=True)
    return arrived.astype(jnp.float32).sum(axis=0)


def together(arrays, axis):
    ends = [0]
    for a in arrays:
        ends.append(ends[-1] + a.size)
    so_far = lax.psum(jnp.concatenate([a.ravel() for a in arrays]), axis)
    return tuple((so_far[b:e].reshape(a.shape) for a, b, e in zip(arrays, ends, ends[1:])))


def layer_norm(rows_in, gain, shift):
    row_mean = jnp.mean(rows_in, axis=-1, keepdims=True)
    centered = rows_in - row_mean
    variance = jnp.mean(centered * centered, axis=-1, keepdims=True)
    return centered * lax.rsqrt(variance + EPSILON) * gain + shift


def exact_gelu(values_in):
    return jax.nn.gelu(values_in, approximate=False)


def choose(onehot, tensor_in):
    return jnp.einsum(
        "sa,a...->s...", onehot, tensor_in, preferred_element_type=jnp.float32
    ).astype(jnp.bfloat16)


def spread(onehot, grads_in):
    return jnp.einsum("sa,s...->a...", onehot, grads_in, precision=HIGHEST)


def seq_dot(left_side, right_side):
    return jnp.einsum("slk,skn->sln", left_side, right_side, preferred_element_type=jnp.float32)


def seq_dot_back(left_side, right_side):
    return jnp.einsum("sln,skn->slk", left_side, right_side, preferred_element_type=jnp.float32)


def seq_outer(left_side, right_side):
    return jnp.einsum("slk,sln->skn", left_side, right_side, preferred_element_type=jnp.float32)


def dot_back(left_side, right_side):
    return lax.dot_general(
        left_side, right_side, (((1,), (1,)), ((), ())), preferred_element_type=jnp.float32
    )


def widen_rows(low_rows):
    seq_total = low_rows.shape[0]
    identity = jnp.eye(seq_total, dtype=low_rows.dtype)
    widened = jnp.einsum("slr,st->sltr", low_rows, identity)
    return widened.reshape(seq_total * low_rows.shape[1], seq_total * low_rows.shape[2])


def block_scores(queries, keys_all, slopes, offset, block_rows):
    length = keys_all.shape[0]
    row_ids = offset + jnp.arange(block_rows)
    distance = (row_ids[:, None] - jnp.arange(length)[None, :]).astype(jnp.float32)
    query_block = lax.dynamic_slice_in_dim(queries, offset, block_rows, 0)
    raw_scores = jnp.einsum(
        "qhe,khe->hqk", query_block, keys_all, preferred_element_type=jnp.float32
    )
    scaled = (raw_scores - slopes[:, None, None] * distance[None]) * 0.125
    return (jnp.where(distance[None] >= 0, scaled, MASKED), query_block)


def attend(queries, keys_all, values_all, slopes, block_rows):
    length = queries.shape[0]

    def one_block(block_index):
        scores, _ = block_scores(queries, keys_all, slopes, block_index * block_rows, block_rows)
        row_max = jnp.max(scores, axis=-1, keepdims=True)
        exp_scores = jnp.exp(scores - row_max)
        row_sum = jnp.sum(exp_scores, axis=-1, keepdims=True)
        attn_probs = (exp_scores / row_sum).astype(jnp.bfloat16)
        context = jnp.einsum(
            "hqk,khe->qhe", attn_probs, values_all, preferred_element_type=jnp.float32
        )
        return (context.astype(jnp.bfloat16), (row_max + jnp.log(row_sum))[..., 0])

    context, log_sums = lax.map(one_block, jnp.arange(length // block_rows))
    return (context.reshape(queries.shape), log_sums)


def attend_back(queries, keys_all, values_all, grad_context, log_sums, slopes, block_rows):
    length = queries.shape[0]

    def one_block(running, block_index):
        grad_keys, grad_values = running
        offset = block_index * block_rows
        scores, query_block = block_scores(queries, keys_all, slopes, offset, block_rows)
        grad_block = lax.dynamic_slice_in_dim(grad_context, offset, block_rows, 0)
        attn_probs = jnp.exp(scores - log_sums[block_index][:, :, None])
        grad_probs = jnp.einsum(
            "qhe,khe->hqk", grad_block, values_all, preferred_element_type=jnp.float32
        )
        row_dot = jnp.sum(attn_probs * grad_probs, axis=-1, keepdims=True)
        grad_scores = (attn_probs * (grad_probs - row_dot)).astype(jnp.bfloat16)
        grad_queries = (
            jnp.einsum("hqk,khe->qhe", grad_scores, keys_all, preferred_element_type=jnp.float32)
            * 0.125
        )
        grad_keys = (
            grad_keys
            + jnp.einsum(
                "hqk,qhe->khe", grad_scores, query_block, preferred_element_type=jnp.float32
            )
            * 0.125
        )
        grad_values = grad_values + jnp.einsum(
            "hqk,qhe->khe",
            attn_probs.astype(jnp.bfloat16),
            grad_block,
            preferred_element_type=jnp.float32,
        )
        return ((grad_keys, grad_values), grad_queries)

    zeros_kv = jnp.zeros(keys_all.shape, jnp.float32)
    (grad_keys, grad_values), grad_queries = lax.scan(
        one_block, (zeros_kv, zeros_kv), jnp.arange(length // block_rows)
    )
    return (grad_queries.reshape(queries.shape), grad_keys, grad_values)


def local(
    tokens,
    grad_out,
    adapter_ids,
    first_gain,
    first_shift,
    joined_weight,
    joined_bias,
    dense_weight,
    dense_bias,
    second_gain,
    second_shift,
    up_weight,
    up_bias,
    down_weight,
    down_bias,
    joined_adapt_in,
    joined_adapt_out,
    dense_adapt_in,
    dense_adapt_out,
    up_adapt_in,
    up_adapt_out,
    down_adapt_in,
    down_adapt_out,
):
    local_rows = tokens.shape[0]
    model_width = tokens.shape[1]
    seq_total = adapter_ids.shape[0]
    group_rows = local_rows * lax.axis_size("tp")
    length = group_rows // seq_total
    block_rows = min(512, length)
    set_count = joined_adapt_in.shape[0]
    low_rank = joined_adapt_in.shape[2]
    joined_width = joined_bias.shape[0]
    hidden_width = up_bias.shape[0]
    local_heads = joined_width // (3 * HEAD_DIM)
    head_cols = local_heads * HEAD_DIM
    head_ids = lax.axis_index("tp") * local_heads + jnp.arange(local_heads)
    slopes = jnp.exp2(-8.0 * (head_ids + 1).astype(jnp.float32) / HEADS)
    matches = adapter_ids[:, None] == jnp.arange(set_count)[None, :]
    onehot_low = matches.astype(jnp.bfloat16)
    onehot_high = matches.astype(jnp.float32)
    pick_joined_in = choose(onehot_low, joined_adapt_in)
    pick_joined_out = choose(onehot_low, joined_adapt_out)
    pick_dense_in = choose(onehot_low, dense_adapt_in)
    pick_dense_out = choose(onehot_low, dense_adapt_out)
    pick_up_in = choose(onehot_low, up_adapt_in)
    pick_up_out = choose(onehot_low, up_adapt_out)
    pick_down_in = choose(onehot_low, down_adapt_in)
    pick_down_out = choose(onehot_low, down_adapt_out)
    residual_in = tokens.astype(jnp.float32)
    normed_one = layer_norm(residual_in, first_gain, first_shift).astype(jnp.bfloat16)
    gathered_one = lax.all_gather(normed_one, "tp", axis=0, tiled=True)
    w_joined, w_dense = (
        lax.all_gather(joined_weight, "fsdp", axis=0, tiled=True),
        lax.all_gather(dense_weight, "fsdp", axis=1, tiled=True),
    )
    seq_one = gathered_one.reshape(seq_total, length, model_width)
    low_joined = seq_dot(seq_one, pick_joined_in).astype(jnp.bfloat16)
    joined_cols = jnp.dot(gathered_one, w_joined, preferred_element_type=jnp.float32).reshape(
        seq_total, length, joined_width
    )
    joined_cols = (joined_cols + seq_dot(low_joined, pick_joined_out) + joined_bias).astype(
        jnp.bfloat16
    )
    joined_heads = joined_cols.reshape(seq_total, length, local_heads, 3, HEAD_DIM)
    sequence = 0
    context, log_sums = attend(
        joined_heads[sequence, :, :, 0, :],
        joined_heads[sequence, :, :, 1, :],
        joined_heads[sequence, :, :, 2, :],
        slopes,
        block_rows,
    )
    contexts = [context]
    log_list = [log_sums]
    seq_context = jnp.stack(contexts).reshape(seq_total, length, head_cols)
    context_rows = seq_context.reshape(group_rows, head_cols)
    low_dense = seq_dot(seq_context, pick_dense_in).astype(jnp.bfloat16)
    wide_dense = widen_rows(low_dense)
    stack_dense = pick_dense_out.reshape(seq_total * low_rank, model_width)
    rows_low = wide_dense
    attn_sum = sum_at_owner(
        (
            jnp.dot(context_rows, w_dense, preferred_element_type=jnp.float32)
            + jnp.dot(rows_low, stack_dense, preferred_element_type=jnp.float32)
        ).astype(jnp.bfloat16),
        "tp",
        0,
    )
    residual_mid = residual_in + attn_sum + dense_bias
    normed_two = layer_norm(residual_mid, second_gain, second_shift).astype(jnp.bfloat16)
    gathered_two = lax.all_gather(normed_two, "tp", axis=0, tiled=True)
    w_up, w_down = (
        lax.all_gather(up_weight, "fsdp", axis=0, tiled=True),
        lax.all_gather(down_weight, "fsdp", axis=1, tiled=True),
    )
    seq_two = gathered_two.reshape(seq_total, length, model_width)
    low_up = seq_dot(seq_two, pick_up_in).astype(jnp.bfloat16)
    pre_act = (
        jnp.dot(gathered_two, w_up, preferred_element_type=jnp.float32)
        + seq_dot(low_up, pick_up_out).reshape(group_rows, hidden_width)
        + up_bias
    )
    activated = exact_gelu(pre_act).astype(jnp.bfloat16)
    seq_act = activated.reshape(seq_total, length, hidden_width)
    low_down = seq_dot(seq_act, pick_down_in).astype(jnp.bfloat16)
    wide_down = widen_rows(low_down)
    stack_down = pick_down_out.reshape(seq_total * low_rank, model_width)
    rows_low = wide_down
    mlp_sum = sum_at_owner(
        (
            jnp.dot(activated, w_down, preferred_element_type=jnp.float32)
            + jnp.dot(rows_low, stack_down, preferred_element_type=jnp.float32)
        ).astype(jnp.bfloat16),
        "tp",
        0,
    )
    layer_out = (residual_mid + mlp_sum + down_bias).astype(jnp.bfloat16)
    grad_mlp = lax.all_gather(grad_out, "tp", axis=0, tiled=True)
    back_up, back_down = (w_up, w_down)
    seq_grad_mlp = grad_mlp.reshape(seq_total, length, model_width)
    grad_low_down = seq_dot_back(seq_grad_mlp, pick_down_out).astype(jnp.bfloat16)
    term_down_out = seq_outer(low_down, seq_grad_mlp)
    term_down_in = seq_outer(seq_act, grad_low_down)
    grad_act = dot_back(grad_mlp, back_down) + seq_dot_back(grad_low_down, pick_down_in).reshape(
        group_rows, hidden_width
    )
    _, gelu_pull = jax.vjp(exact_gelu, pre_act)
    grad_pre = gelu_pull(grad_act)[0].astype(jnp.bfloat16)
    seq_grad_pre = grad_pre.reshape(seq_total, length, hidden_width)
    grad_low_up = seq_dot_back(seq_grad_pre, pick_up_out).astype(jnp.bfloat16)
    term_up_out = seq_outer(low_up, seq_grad_pre)
    term_up_in = seq_outer(seq_two, grad_low_up)
    wide_up = widen_rows(grad_low_up)
    stack_up = jnp.swapaxes(pick_up_in, 1, 2).reshape(seq_total * low_rank, model_width)
    rows_grad = grad_pre
    rows_low = wide_up
    grad_norm_two = sum_at_owner(
        (
            dot_back(rows_grad, back_up)
            + jnp.dot(rows_low, stack_up, preferred_element_type=jnp.float32)
        ).astype(jnp.bfloat16),
        "tp",
        0,
    )
    _, norm_pull_two = jax.vjp(
        lambda rows_in: layer_norm(rows_in, second_gain, second_shift), residual_mid
    )
    grad_mid = grad_out.astype(jnp.float32) + norm_pull_two(grad_norm_two)[0]
    grad_attn = lax.all_gather(grad_mid.astype(jnp.bfloat16), "tp", axis=0, tiled=True)
    back_joined, back_dense = (w_joined, w_dense)
    seq_grad_attn = grad_attn.reshape(seq_total, length, model_width)
    grad_low_dense = seq_dot_back(seq_grad_attn, pick_dense_out).astype(jnp.bfloat16)
    term_dense_out = seq_outer(low_dense, seq_grad_attn)
    term_dense_in = seq_outer(seq_context, grad_low_dense)
    grad_context = dot_back(grad_attn, back_dense) + seq_dot_back(
        grad_low_dense, pick_dense_in
    ).reshape(group_rows, head_cols)
    grad_context = grad_context.astype(jnp.bfloat16).reshape(
        seq_total, length, local_heads, HEAD_DIM
    )
    sequence = 0
    grad_query, grad_key, grad_value = attend_back(
        joined_heads[sequence, :, :, 0, :],
        joined_heads[sequence, :, :, 1, :],
        joined_heads[sequence, :, :, 2, :],
        grad_context[sequence],
        log_list[sequence],
        slopes,
        block_rows,
    )
    grad_parts = [jnp.stack((grad_query, grad_key, grad_value), axis=2)]
    grad_joined = (
        jnp.stack(grad_parts).astype(jnp.bfloat16).reshape(seq_total, length, joined_width)
    )
    grad_low_joined = seq_dot_back(grad_joined, pick_joined_out).astype(jnp.bfloat16)
    term_joined_out = seq_outer(low_joined, grad_joined)
    term_joined_in = seq_outer(seq_one, grad_low_joined)
    grad_joined_rows = grad_joined.reshape(group_rows, joined_width)
    wide_joined = widen_rows(grad_low_joined)
    stack_joined = jnp.swapaxes(pick_joined_in, 1, 2).reshape(seq_total * low_rank, model_width)
    rows_grad = grad_joined_rows
    rows_low = wide_joined
    grad_norm_one = sum_at_owner(
        (
            dot_back(rows_grad, back_joined)
            + jnp.dot(rows_low, stack_joined, preferred_element_type=jnp.float32)
        ).astype(jnp.bfloat16),
        "tp",
        0,
    )
    _, norm_pull_one = jax.vjp(
        lambda rows_in: layer_norm(rows_in, first_gain, first_shift), residual_in
    )
    grad_tokens = grad_mid + norm_pull_one(grad_norm_one)[0]
    wide_sums = tuple(
        (
            part.astype(jnp.float32)
            for part in together(
                (
                    spread(onehot_high, term_joined_out).astype(jnp.bfloat16),
                    spread(onehot_high, term_dense_in).astype(jnp.bfloat16),
                    spread(onehot_high, term_up_out).astype(jnp.bfloat16),
                    spread(onehot_high, term_down_in).astype(jnp.bfloat16),
                ),
                "fsdp",
            )
        )
    )
    both_sums = lax.psum(
        (
            spread(onehot_high, term_joined_in),
            spread(onehot_high, term_dense_out),
            spread(onehot_high, term_up_in),
            spread(onehot_high, term_down_out),
        ),
        ("fsdp", "tp"),
    )
    return (
        layer_out,
        grad_tokens,
        both_sums[0],
        wide_sums[0],
        wide_sums[1],
        both_sums[1],
        both_sums[2],
        wide_sums[2],
        wide_sums[3],
        both_sums[3],
    )


def solution(mesh):
    return jax.shard_map(
        local,
        mesh=mesh,
        in_specs=(
            P(("fsdp", "tp"), None),
            P(("fsdp", "tp"), None),
            P("fsdp"),
            P(),
            P(),
            P("fsdp", "tp"),
            P("tp"),
            P("tp", "fsdp"),
            P(),
            P(),
            P(),
            P("fsdp", "tp"),
            P("tp"),
            P("tp", "fsdp"),
            P(),
            P(),
            P(None, None, "tp"),
            P(None, "tp", None),
            P(),
            P(),
            P(None, None, "tp"),
            P(None, "tp", None),
            P(),
        ),
        out_specs=(
            P(("fsdp", "tp"), None),
            P(("fsdp", "tp"), None),
            P(),
            P(None, None, "tp"),
            P(None, "tp", None),
            P(),
            P(),
            P(None, None, "tp"),
            P(None, "tp", None),
            P(),
        ),
        check_vma=False,
    )
```

profile of v0, /device:TPU:1, one launch (start us, length us, event | category | flops | bytes accessed | tf_op | source)
XLA Modules:
  0.0 977.7 jit_solution(4659292120763606901)
XLA Ops:
  19.2 68.6 %all-gather.9.cloned.1.call-done = bf16[1024,2048]{1,0:T(8,128)(2,1)} async-done(((bf16[128,2048]{1,0:T(8,128)(2,1)}), bf16[1024,2048]{1,0:T(8,128)(2,1)}) %all-gather.9.cloned.1.call-update) | async-done | bytes 4194320 | tf_op jit(solution)/shard_map/all_gather | solution.py:200
  91.2 32.7 %all-gather.11.cloned.1.call-done = bf16[2048,768]{1,0:T(8,128)(2,1)} async-done(((bf16[128,768]{1,0:T(8,128)(2,1)}), bf16[2048,768]{1,0:T(8,128)(2,1)}) %all-gather.11.cloned.1.call-update) | async-done | bytes 3145744 | tf_op jit(solution)/shard_map/all_gather | solution.py:202
  123.9 6.4 fusion.96
  131.2 22.1 %while.28 = (s32[]{:T(128)}, bf16[2,512,4,64]{1,3,2,0:T(8,128)(2,1)S(1)}, f32[2,4,512]{2,1,0:T(4,128)S(1)}, s32[2]{0:T(128)S(1)}, bf16[1024,4,64]{0,2,1:T(8,128)...) while((s32[]{:T(128)}, ...), condition=%wide.region_5.6_spmd.clone, body=%wide.region_2.5_spmd.clone.sunk | while | flops 577370624 | bytes 37297388 | solution.py:104
  154.2 5.4 all-gather.13.cloned.1.call-done
  163.4 62.2 %all_to_all.20 = bf16[8,128,2048]{2,1,0:T(8,128)(2,1)S(1)} all-to-all(bf16[8,128,2048]{2,1,0:T(8,128)(2,1)S(1)} %bitcast.233), channel_id=1, replica_groups=mesh['fsdp'=16,'tp'=8] {'tp'}, dimensions={0} | all-to-all | bytes 8388608 | tf_op jit(solution)/shard_map/all_to_all | solution.py:20
  232.0 33.0 %all-gather.21.cloned.1.call-done = bf16[1024,2048]{1,0:T(8,128)(2,1)} async-done(((bf16[128,2048]{1,0:T(8,128)(2,1)}), bf16[1024,2048]{1,0:T(8,128)(2,1)}) %all-gather.21.cloned.1.call-update) | async-done | bytes 4194320 | tf_op jit(solution)/shard_map/all_gather | solution.py:267
  268.3 41.9 %all-gather.19.cloned.1.call-done = bf16[1024,2048]{1,0:T(8,128)(2,1)} async-done(((bf16[1024,128]{1,0:T(8,128)(2,1)}), bf16[1024,2048]{1,0:T(8,128)(2,1)}) %all-gather.19.cloned.1.call-update) | async-done | bytes 4194320 | tf_op jit(solution)/shard_map/all_gather | solution.py:243
  310.2 10.0 %fusion.100 = f32[1024,1024]{1,0:T(8,128)} fusion(bf16[1024,2048]{1,0:T(8,128)(2,1)} %all-gather.21.cloned.1.call-done, bf16[1024,2048]{1,0:T(8,128)(2,1)} %all-gather.19.cloned.1.call-done), kind=kOutput, calls=%fused_computation.187 | convolution fusion | flops 4294967296 | bytes 12582912 | tf_op jit(solution)/shard_map/dot_general | solution.py:66
  320.2 63.6 %all-gather.15.cloned.1.call-done = bf16[1024,2048]{1,0:T(8,128)(2,1)} async-done(((bf16[128,2048]{1,0:T(8,128)(2,1)}), bf16[1024,2048]{1,0:T(8,128)(2,1)}) %all-gather.15.cloned.1.call-update) | async-done | bytes 4194320 | tf_op jit(solution)/shard_map/all_gather | solution.py:240
  387.2 34.3 %all-gather.17.cloned.1.call-done = bf16[2048,1024]{1,0:T(8,128)(2,1)} async-done(((bf16[128,1024]{1,0:T(8,128)(2,1)}), bf16[2048,1024]{1,0:T(8,128)(2,1)}) %all-gather.17.cloned.1.call-update) | async-done | bytes 4194320 | tf_op jit(solution)/shard_map/all_gather | solution.py:242
  421.5 7.9 fusion.98
  429.5 11.2 %multiply_convert_fusion.2 = (bf16[1024,1024]{1,0:T(8,128)(2,1)}, f32[1024,1024]{1,0:T(8,128)S(1)}, f32[1024,1024]{1,0:T(8,128)S(1)}) fusion(f32[1024]{0:T(1024)S(1)} %copy-done.56, f32[1024,1024]{1,0:T(8,128)S(1)} %fusion.98, bf16[1024,16]{0,1:T(8,128)(2,1)S(1)} %convolution_convert_fusion.4, bf16[1,16,1024]{2,0,1:T(2,128)(2,1)S(1)} %fusion.66), kind=kOutput, calls=%fused_computation.60 | convolution fusion | flops 103809024 | bytes 14749696 | tf_op jit(solution)/shard_map/slk,skn->sln/dot_general | solution.py:54
  443.6 4.6 fusion.101
  451.5 6.5 all-to-all-start.2
  460.2 6.9 fusion.99
  470.5 36.2 %all-to-all-done.2 = bf16[8,128,2048]{2,1,0:T(8,128)(2,1)} async-done(((bf16[8,128,2048]{2,1,0:T(8,128)(2,1)}), bf16[8,128,2048]{2,1,0:T(8,128)(2,1)}, u32[]{:S(2)}, u32[]{:S(2)}) %all-to-all-start.2) | async-done | bytes 4194336 | tf_op jit(solution)/shard_map/all_to_all | solution.py:20
  506.8 5.1 all-to-all-start.1
  515.2 45.4 %all-to-all-done.1 = bf16[8,128,2048]{2,1,0:T(8,128)(2,1)} async-done(((bf16[8,128,2048]{2,1,0:T(8,128)(2,1)}), bf16[8,128,2048]{2,1,0:T(8,128)(2,1)}, u32[]{:S(2)}, u32[]{:S(2)}) %all-to-all-start.1) | async-done | bytes 4194336 | tf_op jit(solution)/shard_map/all_to_all | solution.py:20
  581.9 55.0 %all-gather.23.cloned.1.call-done = bf16[1024,2048]{1,0:T(8,128)(2,1)} async-done(((bf16[128,2048]{1,0:T(8,128)(2,1)}), bf16[1024,2048]{1,0:T(8,128)(2,1)}) %all-gather.23.cloned.1.call-update) | async-done | bytes 4194320 | tf_op jit(solution)/shard_map/all_gather | solution.py:298
  643.7 29.9 %while.29 = (s32[]{:T(128)}, f32[1024,4,64]{0,2,1:T(8,128)S(1)}, f32[1024,4,64]{0,2,1:T(8,128)S(1)}, bf16[2,512,4,64]{1,3,2,0:T(8,128)(2,1)}, s32[2]{0:T(128)S(1...) while((s32[]{:T(128)}, f32[1024,4,64]{0,2,1:T(8,128)S(1)}, ...), condition=%wide.region_15.16_spmd.clone, body=%wide.region_13.15_spmd.clone.sunk | while | flops 1369307648 | bytes 81836928 | solution.py:142
  679.0 5.4 fusion.103
  699.3 101.2 %all-reduce.4.cloned.1.call-done = bf16[393216]{0:T(1024)(128)(2,1)} async-done(((bf16[393216]{0:T(1024)(128)(2,1)}), bf16[393216]{0:T(1024)(128)(2,1)}) %all-reduce.4.cloned.1.call-update) | async-done | bytes 786448 | tf_op jit(solution)/shard_map/psum | solution.py:28
  818.3 145.4 %all-reduce.6.cloned.1.call-done = (f32[8,2048,16]{1,2,0:T(8,128)}, f32[8,16,2048]{2,1,0:T(8,128)}, f32[8,2048,16]{1,2,0:T(8,128)}, f32[8,16,2048]{2,1,0:T(8,128)}) async-done(((f32[8,2048,16]{1,2,0:T(8,128)}, f32[8,16,2048]{2,1,0:T(8,128)}, f32[8,2048,16]{1,2,0:T(8,128)}, f32[8,16,2048]{2,1,0:T(8,128)}), (f32[8,2048,16]{1,2,0:T(8,128)}, f32[8,16,2048]{2,1,0:T(8,128)}, f32[8,2048,16]{1,2,0:T(8,128)}, ...) | async-done | bytes 4194320 | tf_op jit(solution)/shard_map/psum | solution.py:358
  (287 shorter events, 165.3 us)
Async XLA Ops:
  7.2 10.6 %copy-start = (bf16[8,2048,16]{1,2,0:T(8,128)(2,1)S(1)}, bf16[8,2048,16]{1,2,0:T(8,128)(2,1)}, u32[]{:S(2)}) copy-start(bf16[8,2048,16]{1,2,0:T(8,128)(2,1)} %param.42) | copy-start | bytes 1572868
  7.2 11.3 %copy-start.38 = (bf16[8,16,768]{2,1,0:T(8,128)(2,1)S(1)}, bf16[8,16,768]{2,1,0:T(8,128)(2,1)}, u32[]{:S(2)}) copy-start(bf16[8,16,768]{2,1,0:T(8,128)(2,1)} %param.43) | copy-start | bytes 589828
  7.2 11.5 %copy-start.24 = (bf16[8,16,2048]{2,1,0:T(8,128)(2,1)S(1)}, bf16[8,16,2048]{2,1,0:T(8,128)(2,1)}, u32[]{:S(2)}) copy-start(bf16[8,16,2048]{2,1,0:T(8,128)(2,1)} %param.45) | copy-start | bytes 1572868
  7.2 80.6 %all-gather.9.cloned.1.call-start = ((), (), s32[]{:S(2)}) async-start(), calls=%async_computation.4 | async-start | bytes 4718592 | tf_op jit(solution)/shard_map/all_gather | solution.py:200
  13.3 110.7 %all-gather.11.cloned.1.call-start = ((), (), s32[]{:S(2)}) async-start(), calls=%async_computation.5 | async-start | bytes 3342336 | tf_op jit(solution)/shard_map/all_gather | solution.py:202
  14.0 145.6 %all-gather.13.cloned.1.call-start = ((), (), s32[]{:S(2)}) async-start(), calls=%async_computation.6 | async-start | bytes 1114112 | tf_op jit(solution)/shard_map/all_gather | solution.py:203
  14.7 250.2 %all-gather.21.cloned.1.call-start = ((), (), s32[]{:S(2)}) async-start(), calls=%async_computation.10 | async-start | bytes 4718592 | tf_op jit(solution)/shard_map/all_gather | solution.py:267
  15.3 294.9 %all-gather.19.cloned.1.call-start = ((), (), s32[]{:S(2)}) async-start(), calls=%async_computation.9 | async-start | bytes 4456448 | tf_op jit(solution)/shard_map/all_gather | solution.py:243
  15.9 367.9 %all-gather.15.cloned.1.call-start = ((), (), s32[]{:S(2)}) async-start(), calls=%async_computation.7 | async-start | bytes 4718592 | tf_op jit(solution)/shard_map/all_gather | solution.py:240
  18.5 72.6 %copy-start.14 = (bf16[1,2048,16]{2,1,0:T(8,128)(2,1)}, bf16[1,2048,16]{2,1,0:T(8,128)(2,1)S(1)}, u32[]{:S(2)}) copy-start(bf16[1,2048,16]{2,1,0:T(8,128)(2,1)S(1)} %copy.49) | copy-start | bytes 196612
  18.7 111.6 %copy-start.36 = (bf16[1,16,768]{2,0,1:T(2,128)(2,1)}, bf16[1,16,768]{2,0,1:T(2,128)(2,1)S(1)}, u32[]{:S(2)}) copy-start(bf16[1,16,768]{2,0,1:T(2,128)(2,1)S(1)} %fusion.68) | copy-start | bytes 73732
  19.2 142.9 %copy-start.28 = (bf16[1,16,2048]{2,0,1:T(2,128)(2,1)}, bf16[1,16,2048]{2,0,1:T(2,128)(2,1)S(1)}, u32[]{:S(2)}) copy-start(bf16[1,16,2048]{2,0,1:T(2,128)(2,1)S(1)} %fusion.60) | copy-start | bytes 196612
  91.1 39.2 %copy-start.30 = (bf16[1024,16]{0,1:T(8,128)(2,1)}, bf16[1024,16]{0,1:T(8,128)(2,1)S(1)}, u32[]{:S(2)}) copy-start(bf16[1024,16]{0,1:T(8,128)(2,1)S(1)} %convolution_convert_fusion.5) | copy-start | bytes 98308
  91.1 39.2 %copy-start.50 = (f32[768]{0:T(1024)S(1)}, f32[768]{0:T(1024)}, u32[]{:S(2)}) copy-start(f32[768]{0:T(1024)} %param.33) | copy-start | bytes 9220
  228.3 193.3 %all-gather.17.cloned.1.call-start = ((), (), s32[]{:S(2)}) async-start(), calls=%async_computation.8 | async-start | bytes 4456448 | tf_op jit(solution)/shard_map/all_gather | solution.py:242
  387.2 42.3 %copy-start.56 = (f32[1024]{0:T(1024)S(1)}, f32[1024]{0:T(1024)}, u32[]{:S(2)}) copy-start(f32[1024]{0:T(1024)} %param.39) | copy-start | bytes 12292
  429.5 11.2 %copy-start.57 = (f32[1024,1024]{1,0:T(8,128)S(1)}, f32[1024,1024]{1,0:T(8,128)}, u32[]{:S(2)}) copy-start(f32[1024,1024]{1,0:T(8,128)} %fusion.100) | copy-start | bytes 12582916
  451.5 55.3 %all-to-all-start.2 = ((bf16[8,128,2048]{2,1,0:T(8,128)(2,1)}), bf16[8,128,2048]{2,1,0:T(8,128)(2,1)}, u32[]{:S(2)}, u32[]{:S(2)}) async-start(bf16[8,128,2048]{2,1,0:T(8,128)(2,1)} %bitcast.232), calls=%async_computation.2 | async-start | bytes 8388608 | tf_op jit(solution)/shard_map/all_to_all | solution.py:20
  506.8 53.8 %all-to-all-start.1 = ((bf16[8,128,2048]{2,1,0:T(8,128)(2,1)}), bf16[8,128,2048]{2,1,0:T(8,128)(2,1)}, u32[]{:S(2)}, u32[]{:S(2)}) async-start(bf16[8,128,2048]{2,1,0:T(8,128)(2,1)} %bitcast.231), calls=%async_computation.1 | async-start | bytes 8388608 | tf_op jit(solution)/shard_map/all_to_all | solution.py:20
  511.8 125.0 %all-gather.23.cloned.1.call-start = ((), (), s32[]{:S(2)}) async-start(), calls=%async_computation.11 | async-start | bytes 4718592 | tf_op jit(solution)/shard_map/all_gather | solution.py:298
  514.9 48.7 %copy-start.47 = (f32[2048]{0:T(1024)S(1)}, f32[2048]{0:T(1024)}, u32[]{:S(2)}) copy-start(f32[2048]{0:T(1024)} %param.41) | copy-start | bytes 24580
  566.8 233.7 %all-reduce.4.cloned.1.call-start = ((), (), s32[]{:S(2)}) async-start(), calls=%async_computation.12 | async-start | bytes 1572864 | tf_op jit(solution)/shard_map/psum | solution.py:28
  687.7 125.2 %all-to-all-start.3 = ((bf16[8,128,2048]{2,1,0:T(8,128)(2,1)}), bf16[8,128,2048]{2,1,0:T(8,128)(2,1)}, u32[]{:S(2)}, u32[]{:S(2)}) async-start(bf16[8,128,2048]{2,1,0:T(8,128)(2,1)} %bitcast.230), calls=%async_computation.3 | async-start | bytes 8388608 | tf_op jit(solution)/shard_map/all_to_all | solution.py:20
  692.3 271.4 %all-reduce.6.cloned.1.call-start = ((), (), s32[]{:S(2)}) async-start(), calls=%async_computation.13 | async-start | bytes 8388608 | tf_op jit(solution)/shard_map/psum | solution.py:358
  (50 other events, 168.8 us)
Sparse Core Ops, SparseCore 0:
  13.4 74.3 all-gather.8
  89.5 34.3 all-gather.10
  125.5 33.9 all-gather.12
  161.8 103.1 all-gather.20
  266.4 43.7 all-gather.18
  313.0 70.7 all-gather.14
  385.6 35.9 all-gather.16
  566.9 69.9 all-gather.22
  679.1 121.3 all-reduce.3
  807.4 156.1 all-reduce.5
where the time goes:
time: 982 us; the launch traced here: 978 us
  waiting for transfers between devices  666 us (68%)
  matrix products  139 us (14%)
  blocking collectives  62.2 us (6%)
  other arithmetic  40.9 us (4%)
  local copies, waits for them, and re-layouts  29.7 us (3%)
  starting transfers between devices  16.5 us (2%)
  between operations  16.2 us (2%)
    psum x1, waiting for transfers between devices, local(): lax.psum((spread(onehot_high, term_joined_in), spread(onehot_high, term_d...  145 us
    psum x1, waiting for transfers between devices, together(): so_far = lax.psum(jnp.concatenate([a.ravel() for a in arrays]), axis)  101 us
    all_to_all x3, waiting for transfers between devices, sum_at_owner(): lax.all_to_all(blocks, axis, split_axis=0, concat_axis=0, tiled=True)  81.6 us
    all_gather x1, waiting for transfers between devices, local(): gathered_one = lax.all_gather(normed_one, 'tp', axis=0, tiled=True)  68.6 us
    all_gather x1, waiting for transfers between devices, local(): gathered_two = lax.all_gather(normed_two, 'tp', axis=0, tiled=True)  63.6 us
    all_to_all x1, blocking collectives, sum_at_owner(): lax.all_to_all(blocks, axis, split_axis=0, concat_axis=0, tiled=True)  62.2 us
    all_gather x1, waiting for transfers between devices, local(): lax.all_gather(grad_mid.astype(jnp.bfloat16), 'tp', axis=0, tiled=True)  55 us
    all_gather x1, waiting for transfers between devices, local(): lax.all_gather(down_weight, 'fsdp', axis=1, tiled=True)  41.9 us
  transfers between devices with their start and end apart: 13, of which 12 were waited for; matrix products, arithmetic and copies ran while one was open for 13% of the time, Pallas kernels for 0%

commit v1 on v0

--- a/solution.py
+++ b/solution.py
@@ -356,13 +356,16 @@
         )
     )
     both_sums = lax.psum(
-        (
-            spread(onehot_high, term_joined_in),
-            spread(onehot_high, term_dense_out),
-            spread(onehot_high, term_up_in),
-            spread(onehot_high, term_down_out),
+        lax.psum(
+            (
+                spread(onehot_high, term_joined_in),
+                spread(onehot_high, term_dense_out),
+                spread(onehot_high, term_up_in),
+                spread(onehot_high, term_down_out),
+            ),
+            "fsdp",
         ),
-        ("fsdp", "tp"),
+        "tp",
     )
     return (
         layer_out,

time: 982 us -> 1070 us (1.090)
  waiting for transfers between devices: 666 us -> 751 us
    psum x0 -> x1, waiting for transfers between devices: none -> 99.1 us  [local(): lax.psum(lax.psum((spread(onehot_high, term_joined_in), spread(onehot_hig...]
    psum x1, waiting for transfers between devices: 145 us -> 132 us  [local(): lax.psum((spread(onehot_high, term_joined_in), spread(onehot_high, term_d...]
  transfers between devices with their start and end apart: 13 -> 14, of which waited for: 12 -> 13; matrix products, arithmetic and copies ran while one was open for 13% -> 12% of each run, Pallas kernels for 0% -> 0%
where the time goes in v1:
time: 1070 us; the launch traced here: 1060 us
  waiting for transfers between devices  751 us (70%)
  matrix products  139 us (13%)
  blocking collectives  62.2 us (6%)
  other arithmetic  40.9 us (4%)
  local copies, waits for them, and re-layouts  28.5 us (3%)
  starting transfers between devices  16.8 us (2%)
  between operations  15.9 us (1%)
    psum x1, waiting for transfers between devices, local(): lax.psum((spread(onehot_high, term_joined_in), spread(onehot_high, term_d...  132 us
    psum x1, waiting for transfers between devices, together(): so_far = lax.psum(jnp.concatenate([a.ravel() for a in arrays]), axis)  100 us
    psum x1, waiting for transfers between devices, local(): lax.psum(lax.psum((spread(onehot_high, term_joined_in), spread(onehot_hig...  99.1 us
    all_to_all x3, waiting for transfers between devices, sum_at_owner(): lax.all_to_all(blocks, axis, split_axis=0, concat_axis=0, tiled=True)  81.6 us
    all_gather x1, waiting for transfers between devices, local(): gathered_one = lax.all_gather(normed_one, 'tp', axis=0, tiled=True)  68.5 us
    all_gather x1, waiting for transfers between devices, local(): gathered_two = lax.all_gather(normed_two, 'tp', axis=0, tiled=True)  63.6 us
    all_to_all x1, blocking collectives, sum_at_owner(): lax.all_to_all(blocks, axis, split_axis=0, concat_axis=0, tiled=True)  62.2 us
    all_gather x1, waiting for transfers between devices, local(): lax.all_gather(grad_mid.astype(jnp.bfloat16), 'tp', axis=0, tiled=True)  55 us
  transfers between devices with their start and end apart: 14, of which 13 were waited for; matrix products, arithmetic and copies ran while one was open for 12% of the time, Pallas kernels for 0%

profile of v1, /device:TPU:1, one launch (start us, length us, event | category | flops | bytes accessed | tf_op | source)
XLA Modules:
  0.0 1061.4 jit_solution(16100968086034289109)
XLA Ops:
  18.2 68.5 %all-gather.9.cloned.1.call-done = bf16[1024,2048]{1,0:T(8,128)(2,1)} async-done(((bf16[128,2048]{1,0:T(8,128)(2,1)}), bf16[1024,2048]{1,0:T(8,128)(2,1)}) %all-gather.9.cloned.1.call-update) | async-done | bytes 4194320 | tf_op jit(solution)/shard_map/all_gather | solution.py:200
  90.1 32.7 %all-gather.11.cloned.1.call-done = bf16[2048,768]{1,0:T(8,128)(2,1)} async-done(((bf16[128,768]{1,0:T(8,128)(2,1)}), bf16[2048,768]{1,0:T(8,128)(2,1)}) %all-gather.11.cloned.1.call-update) | async-done | bytes 3145744 | tf_op jit(solution)/shard_map/all_gather | solution.py:202
  122.9 6.4 fusion.96
  130.1 22.1 %while.28 = (s32[]{:T(128)}, bf16[2,512,4,64]{1,3,2,0:T(8,128)(2,1)S(1)}, f32[2,4,512]{2,1,0:T(4,128)S(1)}, s32[2]{0:T(128)S(1)}, bf16[1024,4,64]{0,2,1:T(8,128)...) while((s32[]{:T(128)}, ...), condition=%wide.region_5.6_spmd.clone, body=%wide.region_2.5_spmd.clone.sunk | while | flops 577370624 | bytes 37297388 | solution.py:104
  153.1 5.4 all-gather.13.cloned.1.call-done
  162.4 62.2 %all_to_all.20 = bf16[8,128,2048]{2,1,0:T(8,128)(2,1)S(1)} all-to-all(bf16[8,128,2048]{2,1,0:T(8,128)(2,1)S(1)} %bitcast.233), channel_id=1, replica_groups=mesh['fsdp'=16,'tp'=8] {'tp'}, dimensions={0} | all-to-all | bytes 8388608 | tf_op jit(solution)/shard_map/all_to_all | solution.py:20
  231.0 32.9 %all-gather.21.cloned.1.call-done = bf16[1024,2048]{1,0:T(8,128)(2,1)} async-done(((bf16[128,2048]{1,0:T(8,128)(2,1)}), bf16[1024,2048]{1,0:T(8,128)(2,1)}) %all-gather.21.cloned.1.call-update) | async-done | bytes 4194320 | tf_op jit(solution)/shard_map/all_gather | solution.py:267
  267.3 41.9 %all-gather.19.cloned.1.call-done = bf16[1024,2048]{1,0:T(8,128)(2,1)} async-done(((bf16[1024,128]{1,0:T(8,128)(2,1)}), bf16[1024,2048]{1,0:T(8,128)(2,1)}) %all-gather.19.cloned.1.call-update) | async-done | bytes 4194320 | tf_op jit(solution)/shard_map/all_gather | solution.py:243
  309.2 10.0 fusion.100
  319.2 63.6 %all-gather.15.cloned.1.call-done = bf16[1024,2048]{1,0:T(8,128)(2,1)} async-done(((bf16[128,2048]{1,0:T(8,128)(2,1)}), bf16[1024,2048]{1,0:T(8,128)(2,1)}) %all-gather.15.cloned.1.call-update) | async-done | bytes 4194320 | tf_op jit(solution)/shard_map/all_gather | solution.py:240
  386.2 34.3 %all-gather.17.cloned.1.call-done = bf16[2048,1024]{1,0:T(8,128)(2,1)} async-done(((bf16[128,1024]{1,0:T(8,128)(2,1)}), bf16[2048,1024]{1,0:T(8,128)(2,1)}) %all-gather.17.cloned.1.call-update) | async-done | bytes 4194320 | tf_op jit(solution)/shard_map/all_gather | solution.py:242
  420.5 8.0 fusion.98
  428.4 11.2 %multiply_convert_fusion.2 = (bf16[1024,1024]{1,0:T(8,128)(2,1)}, f32[1024,1024]{1,0:T(8,128)S(1)}, f32[1024,1024]{1,0:T(8,128)S(1)}) fusion(f32[1024]{0:T(1024)S(1)} %copy-done.56, f32[1024,1024]{1,0:T(8,128)S(1)} %fusion.98, bf16[1024,16]{0,1:T(8,128)(2,1)S(1)} %convolution_convert_fusion.4, bf16[1,16,1024]{2,0,1:T(2,128)(2,1)S(1)} %fusion.66), kind=kOutput, calls=%fused_computation.60 | convolution fusion | flops 103809024 | bytes 14749696 | tf_op jit(solution)/shard_map/slk,skn->sln/dot_general | solution.py:54
  450.4 6.5 all-to-all-start.2
  459.2 6.9 fusion.99
  469.5 36.2 %all-to-all-done.2 = bf16[8,128,2048]{2,1,0:T(8,128)(2,1)} async-done(((bf16[8,128,2048]{2,1,0:T(8,128)(2,1)}), bf16[8,128,2048]{2,1,0:T(8,128)(2,1)}, u32[]{:S(2)}, u32[]{:S(2)}) %all-to-all-start.2) | async-done | bytes 4194336 | tf_op jit(solution)/shard_map/all_to_all | solution.py:20
  505.7 5.1 all-to-all-start.1
  514.2 45.4 %all-to-all-done.1 = bf16[8,128,2048]{2,1,0:T(8,128)(2,1)} async-done(((bf16[8,128,2048]{2,1,0:T(8,128)(2,1)}), bf16[8,128,2048]{2,1,0:T(8,128)(2,1)}, u32[]{:S(2)}, u32[]{:S(2)}) %all-to-all-start.1) | async-done | bytes 4194336 | tf_op jit(solution)/shard_map/all_to_all | solution.py:20
  580.9 55.0 %all-gather.23.cloned.1.call-done = bf16[1024,2048]{1,0:T(8,128)(2,1)} async-done(((bf16[128,2048]{1,0:T(8,128)(2,1)}), bf16[1024,2048]{1,0:T(8,128)(2,1)}) %all-gather.23.cloned.1.call-update) | async-done | bytes 4194320 | tf_op jit(solution)/shard_map/all_gather | solution.py:298
  642.7 29.7 %while.29 = (s32[]{:T(128)}, f32[1024,4,64]{0,2,1:T(8,128)S(1)}, f32[1024,4,64]{0,2,1:T(8,128)S(1)}, bf16[2,512,4,64]{1,3,2,0:T(8,128)(2,1)}, s32[2]{0:T(128)S(1...) while((s32[]{:T(128)}, f32[1024,4,64]{0,2,1:T(8,128)S(1)}, ...), condition=%wide.region_15.16_spmd.clone, body=%wide.region_13.15_spmd.clone.sunk | while | flops 1369307648 | bytes 81836928 | solution.py:142
  685.0 5.4 fusion.103
  698.4 100.2 %all-reduce.6.cloned.1.call-done = bf16[393216]{0:T(1024)(128)(2,1)} async-done(((bf16[393216]{0:T(1024)(128)(2,1)}), bf16[393216]{0:T(1024)(128)(2,1)}) %all-reduce.6.cloned.1.call-update) | async-done | bytes 786448 | tf_op jit(solution)/shard_map/psum | solution.py:28
  799.6 132.5 %all-reduce.8.cloned.1.call-done = (f32[8,2048,16]{1,2,0:T(8,128)}, f32[8,16,2048]{2,1,0:T(8,128)}, f32[8,2048,16]{1,2,0:T(8,128)}, f32[8,16,2048]{2,1,0:T(8,128)}) async-done(((f32[8,2048,16]{1,2,0:T(8,128)}, f32[8,16,2048]{2,1,0:T(8,128)}, f32[8,2048,16]{1,2,0:T(8,128)}, f32[8,16,2048]{2,1,0:T(8,128)}), (f32[8,2048,16]{1,2,0:T(8,128)}, f32[8,16,2048]{2,1,0:T(8,128)}, f32[8,2048,16]{1,2,0:T(8,128)}, ...) | async-done | bytes 4194320 | tf_op jit(solution)/shard_map/psum | solution.py:359
  948.6 99.1 %all-reduce.10.cloned.1.call-done = (f32[8,2048,16]{1,2,0:T(8,128)}, f32[8,16,2048]{2,1,0:T(8,128)}, f32[8,2048,16]{1,2,0:T(8,128)}, f32[8,16,2048]{2,1,0:T(8,128)}) async-done(((f32[8,2048,16]{1,2,0:T(8,128)}, f32[8,16,2048]{2,1,0:T(8,128)}, f32[8,2048,16]{1,2,0:T(8,128)}, f32[8,16,2048]{2,1,0:T(8,128)}), (f32[8,2048,16]{1,2,0:T(8,128)}, f32[8,16,2048]{2,1,0:T(8,128)}, f32[8,2048,16]{1,2,0:T(8,128)}, ...) | async-done | bytes 4194320 | tf_op jit(solution)/shard_map/psum | solution.py:358
  (290 shorter events, 168.9 us)
Async XLA Ops:
  7.2 10.3 copy-start.38
  7.2 10.5 copy-start.24
  7.2 79.5 %all-gather.9.cloned.1.call-start = ((), (), s32[]{:S(2)}) async-start(), calls=%async_computation.4 | async-start | bytes 4718592 | tf_op jit(solution)/shard_map/all_gather | solution.py:200
  12.2 110.7 %all-gather.11.cloned.1.call-start = ((), (), s32[]{:S(2)}) async-start(), calls=%async_computation.5 | async-start | bytes 3342336 | tf_op jit(solution)/shard_map/all_gather | solution.py:202
  12.9 145.6 %all-gather.13.cloned.1.call-start = ((), (), s32[]{:S(2)}) async-start(), calls=%async_computation.6 | async-start | bytes 1114112 | tf_op jit(solution)/shard_map/all_gather | solution.py:203
  13.7 250.2 %all-gather.21.cloned.1.call-start = ((), (), s32[]{:S(2)}) async-start(), calls=%async_computation.10 | async-start | bytes 4718592 | tf_op jit(solution)/shard_map/all_gather | solution.py:267
  14.3 294.9 %all-gather.19.cloned.1.call-start = ((), (), s32[]{:S(2)}) async-start(), calls=%async_computation.9 | async-start | bytes 4456448 | tf_op jit(solution)/shard_map/all_gather | solution.py:243
  14.8 368.0 %all-gather.15.cloned.1.call-start = ((), (), s32[]{:S(2)}) async-start(), calls=%async_computation.7 | async-start | bytes 4718592 | tf_op jit(solution)/shard_map/all_gather | solution.py:240
  17.5 72.6 %copy-start.14 = (bf16[1,2048,16]{2,1,0:T(8,128)(2,1)}, bf16[1,2048,16]{2,1,0:T(8,128)(2,1)S(1)}, u32[]{:S(2)}) copy-start(bf16[1,2048,16]{2,1,0:T(8,128)(2,1)S(1)} %copy.49) | copy-start | bytes 196612
  17.7 111.6 %copy-start.36 = (bf16[1,16,768]{2,0,1:T(2,128)(2,1)}, bf16[1,16,768]{2,0,1:T(2,128)(2,1)S(1)}, u32[]{:S(2)}) copy-start(bf16[1,16,768]{2,0,1:T(2,128)(2,1)S(1)} %fusion.68) | copy-start | bytes 73732
  18.2 142.9 %copy-start.28 = (bf16[1,16,2048]{2,0,1:T(2,128)(2,1)}, bf16[1,16,2048]{2,0,1:T(2,128)(2,1)S(1)}, u32[]{:S(2)}) copy-start(bf16[1,16,2048]{2,0,1:T(2,128)(2,1)S(1)} %fusion.60) | copy-start | bytes 196612
  90.1 39.2 %copy-start.30 = (bf16[1024,16]{0,1:T(8,128)(2,1)}, bf16[1024,16]{0,1:T(8,128)(2,1)S(1)}, u32[]{:S(2)}) copy-start(bf16[1024,16]{0,1:T(8,128)(2,1)S(1)} %convolution_convert_fusion.5) | copy-start | bytes 98308
  90.1 39.2 %copy-start.50 = (f32[768]{0:T(1024)S(1)}, f32[768]{0:T(1024)}, u32[]{:S(2)}) copy-start(f32[768]{0:T(1024)} %param.33) | copy-start | bytes 9220
  227.2 193.2 %all-gather.17.cloned.1.call-start = ((), (), s32[]{:S(2)}) async-start(), calls=%async_computation.8 | async-start | bytes 4456448 | tf_op jit(solution)/shard_map/all_gather | solution.py:242
  386.2 42.3 %copy-start.56 = (f32[1024]{0:T(1024)S(1)}, f32[1024]{0:T(1024)}, u32[]{:S(2)}) copy-start(f32[1024]{0:T(1024)} %param.39) | copy-start | bytes 12292
  428.4 11.2 %copy-start.57 = (f32[1024,1024]{1,0:T(8,128)S(1)}, f32[1024,1024]{1,0:T(8,128)}, u32[]{:S(2)}) copy-start(f32[1024,1024]{1,0:T(8,128)} %fusion.100) | copy-start | bytes 12582916
  450.4 55.3 %all-to-all-start.2 = ((bf16[8,128,2048]{2,1,0:T(8,128)(2,1)}), bf16[8,128,2048]{2,1,0:T(8,128)(2,1)}, u32[]{:S(2)}, u32[]{:S(2)}) async-start(bf16[8,128,2048]{2,1,0:T(8,128)(2,1)} %bitcast.232), calls=%async_computation.2 | async-start | bytes 8388608 | tf_op jit(solution)/shard_map/all_to_all | solution.py:20
  505.7 53.8 %all-to-all-start.1 = ((bf16[8,128,2048]{2,1,0:T(8,128)(2,1)}), bf16[8,128,2048]{2,1,0:T(8,128)(2,1)}, u32[]{:S(2)}, u32[]{:S(2)}) async-start(bf16[8,128,2048]{2,1,0:T(8,128)(2,1)} %bitcast.231), calls=%async_computation.1 | async-start | bytes 8388608 | tf_op jit(solution)/shard_map/all_to_all | solution.py:20
  510.8 125.0 %all-gather.23.cloned.1.call-start = ((), (), s32[]{:S(2)}) async-start(), calls=%async_computation.11 | async-start | bytes 4718592 | tf_op jit(solution)/shard_map/all_gather | solution.py:298
  513.9 48.7 %copy-start.47 = (f32[2048]{0:T(1024)S(1)}, f32[2048]{0:T(1024)}, u32[]{:S(2)}) copy-start(f32[2048]{0:T(1024)} %param.41) | copy-start | bytes 24580
  565.8 232.8 %all-reduce.6.cloned.1.call-start = ((), (), s32[]{:S(2)}) async-start(), calls=%async_computation.12 | async-start | bytes 1572864 | tf_op jit(solution)/shard_map/psum | solution.py:28
  677.8 254.4 %all-reduce.8.cloned.1.call-start = ((), (), s32[]{:S(2)}) async-start(), calls=%async_computation.13 | async-start | bytes 8388608 | tf_op jit(solution)/shard_map/psum | solution.py:359
  693.7 249.5 %all-to-all-start.3 = ((bf16[8,128,2048]{2,1,0:T(8,128)(2,1)}), bf16[8,128,2048]{2,1,0:T(8,128)(2,1)}, u32[]{:S(2)}, u32[]{:S(2)}) async-start(bf16[8,128,2048]{2,1,0:T(8,128)(2,1)} %bitcast.230), calls=%async_computation.3 | async-start | bytes 8388608 | tf_op jit(solution)/shard_map/all_to_all | solution.py:20
  698.3 349.4 %all-reduce.10.cloned.1.call-start = ((), (), s32[]{:S(2)}) async-start(), calls=%async_computation.14 | async-start | bytes 8388608 | tf_op jit(solution)/shard_map/psum | solution.py:358
  (51 other events, 200.4 us)
Sparse Core Ops, SparseCore 0:
  12.3 74.3 all-gather.8
  88.4 34.3 all-gather.10
  124.5 33.9 all-gather.12
  160.7 103.1 all-gather.20
  265.4 43.7 all-gather.18
  312.0 70.7 all-gather.14
  384.5 35.9 all-gather.16
  565.9 69.9 all-gather.22
  677.9 120.6 all-reduce.5
  801.9 130.1 all-reduce.7
  935.1 112.5 all-reduce.9
